TPU v7x, 32 devices: a whole 2x2x4 slice. The times are simulated.
32 devices in a mesh: pts: 8 (over z, y), grp: 4 (over x, core).
Axes of the slice: x: 2, y: 2, z: 4, core: 2. Of those that a mesh axis runs over, the one named last changes fastest.
Arguments:
- jacobian: bfloat16 [32, 6, 128, 3, 256], P(('pts', 'grp')), may hold values from -0.21875 to 0.21875
- point_blocks: float32 [32, 6, 256], P(('pts', 'grp')), may hold values from -0.5 to 4, as said below
- point_grad: bfloat16 [32, 3, 256], P(('pts', 'grp')), may hold values from -6 to 6
- camera_grad: float32 [32, 128], P(('pts', 'grp')), may hold values from -6 to 6
- damping: float32 [32, 128], replicated, may hold values from 1 to 8
- incidence: int32 [32, 6], P(('pts', 'grp')), may hold values from 0 to 31, as said below
- tile_owner: int32 [8], replicated, may hold values from 0 to 7, each once
- front_first: int32 [1], replicated, may hold values from 0 to 31
Outputs:
- tiles_out: float32 [256, 128, 128], P(('pts', 'grp'))
- rhs_out: float32 [32, 128], P(('pts', 'grp'))
- front_panel: float32 [2304, 512], P(None, 'grp')
Inputs may be any that keep to these rules, and one draw needn't show every extreme that they name: `incidence`: point cluster p names 6 different camera clusters, all among (p + t) mod 32 for t from 0 to 7. `point_blocks`: each point's diagonal entries exceed the sum of the magnitudes of the two off-diagonal entries of their row by 0.1 or more. `tile_owner`: A permutation of the pts indices.
All inputs are finite; a program needn't handle non-finite values.
Results may differ from a plain program's by a relative error of at most 0.0022.
Values sent between devices are 32-bit elements; how exact they have to be, the bound alone decides.
No kernel may reach another device: no remote copies, remote signals or barrier semaphores. Data moves between devices by JAX's collectives and lax.ppermute only.
A program may use at most 128 MiB of HBM per device.

v0:
```python
import jax
import jax.numpy as jnp
import numpy as np
from jax import lax
from jax.sharding import PartitionSpec as P

TOUCH = 6
BAND = 8
FRONT = 4
PRECISE = lax.Precision.HIGHEST


def shifted(value, axis, steps):
    count = lax.axis_size(axis)
    pairs = [(source, (source + steps) % count) for source in range(count)]
    return lax.ppermute(value, axis, pairs)


def invert_blocks(blocks):
    diag_x = blocks[:, 0]
    diag_y = blocks[:, 1]
    diag_z = blocks[:, 2]
    cross_xy = blocks[:, 3]
    cross_xz = blocks[:, 4]
    cross_yz = blocks[:, 5]
    adj_xx = diag_y * diag_z - cross_yz * cross_yz
    adj_yy = diag_x * diag_z - cross_xz * cross_xz
    adj_zz = diag_x * diag_y - cross_xy * cross_xy
    adj_xy = cross_xz * cross_yz - cross_xy * diag_z
    adj_xz = cross_xy * cross_yz - diag_y * cross_xz
    adj_yz = cross_xy * cross_xz - diag_x * cross_yz
    determinant = diag_x * adj_xx + cross_xy * adj_xy + cross_xz * adj_xz
    inverse_det = 1.0 / determinant
    return [
        [adj_xx * inverse_det, adj_xy * inverse_det, adj_xz * inverse_det],
        [adj_xy * inverse_det, adj_yy * inverse_det, adj_yz * inverse_det],
        [adj_xz * inverse_det, adj_yz * inverse_det, adj_zz * inverse_det],
    ]


def scale_jacobian(jacobian, blocks):
    inverse = invert_blocks(blocks)
    widened = jacobian.astype(jnp.float32)
    columns = []
    for target in range(3):
        summed = widened[:, :, :, 0, :] * inverse[0][target][:, None, None, :]
        summed = summed + widened[:, :, :, 1, :] * inverse[1][target][:, None, None, :]
        summed = summed + widened[:, :, :, 2, :] * inverse[2][target][:, None, None, :]
        columns.append(summed)
    return jnp.stack(columns, axis=3).astype(jnp.bfloat16)


def band_table(reach_rows, reach_sum):
    row_list = []
    offset_list = []
    for row_pos in range(reach_rows):
        for offset in range(BAND):
            if row_pos + offset <= reach_sum:
                row_list.append(row_pos)
                offset_list.append(offset)
    return (np.array(row_list), np.array(offset_list))


def route_rows(tiles, tile_owner, base, row_list, offset_list, pts_count):
    offsets = BAND * row_list + offset_list
    capacity = int(offsets.max()) // pts_count + 1
    residue = jnp.mod(base + jnp.asarray(offsets), pts_count)
    target = tile_owner[residue] * capacity + jnp.asarray(offsets // pts_count)
    sending = (jnp.arange(pts_count * capacity)[:, None] == target[None, :]).astype(jnp.float32)
    return (jnp.einsum("dt,trc->drc", sending, tiles, precision=PRECISE), capacity)


def collect_rows(
    incoming, capacity, perm_inverse, anchors, usable_test, clusters, grp_count, pts_count
):
    sender = jnp.arange(pts_count * capacity) // capacity
    slot_of = jnp.arange(pts_count * capacity) % capacity
    sender_anchor = anchors(sender)
    arrived = jnp.mod(perm_inverse - BAND * sender_anchor, pts_count) + slot_of * pts_count
    row_pos = arrived // BAND
    offset = arrived % BAND
    usable = usable_test(row_pos, offset)
    home_row = jnp.mod(sender_anchor + row_pos, clusters)
    owner_slot = (BAND * home_row + offset) // pts_count
    gathering = (
        (jnp.arange(BAND * grp_count)[:, None] == owner_slot[None, :]) & usable[None, :]
    ).astype(jnp.float32)
    return jnp.einsum("ms,src->mrc", gathering, incoming, precision=PRECISE)


def per_device(
    jacobian, point_blocks, point_grad, camera_grad, damping, incidence, tile_owner, front_first
):
    pts_count = lax.axis_size("pts")
    grp_count = lax.axis_size("grp")
    clusters = pts_count * grp_count
    my_grp = lax.axis_index("grp")
    my_pts = lax.axis_index("pts")
    device = my_pts * grp_count + my_grp
    local_count = jacobian.shape[0]
    cam_rows = jacobian.shape[2]
    point_cols = 3 * jacobian.shape[4]
    window_len = 2 * BAND - 2 + FRONT
    reach = 2 * BAND - 1
    scaled = scale_jacobian(jacobian, point_blocks).reshape(
        local_count, TOUCH, cam_rows, point_cols
    )
    jac_flat = jacobian.reshape(local_count, TOUCH, cam_rows, point_cols)
    local_slot = jnp.mod(incidence - device, clusters)
    placing = (local_slot[:, None, :] == jnp.arange(BAND)[None, :, None]).astype(jnp.bfloat16)
    placed_scaled = jnp.einsum(
        "ptk,pkrx->ptrx", placing, scaled, preferred_element_type=jnp.float32
    ).astype(jnp.bfloat16)
    placed_jac = jnp.einsum(
        "ptk,pkrx->ptrx", placing, jac_flat, preferred_element_type=jnp.float32
    ).astype(jnp.bfloat16)
    band_grid = jnp.einsum(
        "ptrx,pqcx->tqrc", placed_scaled, placed_jac, preferred_element_type=jnp.float32
    )
    band_rhs = jnp.einsum(
        "ptrx,px->tr",
        placed_scaled,
        point_grad.reshape(local_count, point_cols),
        preferred_element_type=jnp.float32,
    )
    perm_inverse = jnp.sum(jnp.arange(pts_count) * (tile_owner == my_pts))
    row_list, offset_list = band_table(BAND, BAND - 1)
    band_tiles = band_grid[row_list, row_list + offset_list]
    quarters = lax.all_to_all(band_tiles, "grp", split_axis=1, concat_axis=0, tiled=True)
    reach_union = BAND + grp_count - 2
    union_rows_list, union_offsets = band_table(reach_union + 1, reach_union)
    lookup = {}
    for position in range(len(union_rows_list)):
        lookup[int(union_rows_list[position]), int(union_offsets[position])] = position
    merge_table = np.zeros((len(union_rows_list), grp_count * len(row_list)), np.float32)
    for source_grp in range(grp_count):
        for position in range(len(row_list)):
            merge_table[
                lookup[source_grp + int(row_list[position]), int(offset_list[position])],
                source_grp * len(row_list) + position,
            ] = 1.0
    union_rows = jnp.einsum("us,src->urc", jnp.asarray(merge_table), quarters, precision=PRECISE)
    outgoing, capacity = route_rows(
        union_rows, tile_owner, BAND * grp_count * my_pts, union_rows_list, union_offsets, pts_count
    )
    incoming = lax.all_to_all(outgoing, "pts", split_axis=0, concat_axis=0, tiled=True)
    owner_rows = collect_rows(
        incoming,
        capacity,
        perm_inverse,
        lambda sender: sender * grp_count,
        lambda row_pos, offset: row_pos + offset <= reach_union,
        clusters,
        grp_count,
        pts_count,
    )
    owned = lax.all_to_all(owner_rows, "grp", split_axis=0, concat_axis=1, tiled=True)
    tile_id = perm_inverse + pts_count * (BAND * my_grp + jnp.arange(BAND))
    home_row = tile_id // BAND
    offset = tile_id % BAND
    other_row = jnp.mod(home_row + offset, clusters)
    pick_damp = (home_row[:, None] == jnp.arange(clusters)[None, :]).astype(jnp.float32)
    damp_rows = jnp.dot(pick_damp, damping, precision=PRECISE)
    identity = jnp.eye(cam_rows, dtype=jnp.float32)
    owned = owned + jnp.where(
        (offset == 0)[:, None, None], damp_rows[:, :, None] * identity[None, :, :], 0.0
    )
    summed = band_rhs[0]
    for step in range(1, BAND):
        summed = summed + shifted(band_rhs[step], ("pts", "grp"), step)
    reduced = camera_grad - summed[None, :]
    front_start = front_first[0]
    window_base = front_start - (BAND - 1)
    pos_home = jnp.mod(home_row - window_base, clusters)
    pos_other = jnp.mod(other_row - window_base, clusters)
    front_axis = jnp.arange(FRONT)[:, None, None]
    reach_axis = jnp.arange(reach)[None, :, None]
    direct = (
        (pos_other[None, None, :] == BAND - 1 + front_axis)
        & (pos_home[None, None, :] == front_axis + reach_axis)
    ).astype(jnp.float32)
    mirror = (
        (pos_home[None, None, :] == BAND - 1 + front_axis)
        & (offset[None, None, :] > 0)
        & (pos_other[None, None, :] == front_axis + reach_axis)
    ).astype(jnp.float32)
    front_rows = jnp.einsum("kes,sab->keab", direct, owned, precision=PRECISE) + jnp.einsum(
        "kes,sba->keab", mirror, owned, precision=PRECISE
    )
    my_pos = jnp.mod(device - window_base, clusters)
    window_rhs = (jnp.arange(window_len)[:, None] == my_pos).astype(jnp.float32) * reduced
    front_rows, window_rhs = lax.psum((front_rows, window_rhs), ("pts", "grp"))
    flat_rows = jnp.concatenate(
        [
            front_rows.reshape(FRONT * reach, cam_rows, cam_rows),
            jnp.zeros((1, cam_rows, cam_rows), jnp.float32),
        ],
        axis=0,
    )
    lookup_table = np.full((window_len, FRONT), FRONT * reach, np.int32)
    for position in range(window_len):
        for front_pos in range(FRONT):
            if 0 <= position - front_pos < reach:
                lookup_table[position, front_pos] = front_pos * reach + position - front_pos
    columns = (
        flat_rows[lookup_table]
        .transpose(0, 2, 1, 3)
        .reshape(window_len * cam_rows, FRONT * cam_rows)
    )
    square = columns[(BAND - 1) * cam_rows : (BAND - 1 + FRONT) * cam_rows]
    factor = jnp.linalg.cholesky(square)
    panel = jax.scipy.linalg.solve_triangular(factor, columns.T, lower=True).T
    share = FRONT * cam_rows // grp_count
    front_panel = lax.dynamic_slice_in_dim(panel, my_grp * share, share, 1)
    panel_blocks = panel.reshape(window_len, cam_rows, FRONT * cam_rows)

    def inside_rest(position):
        return (position < window_len) & ((position < BAND - 1) | (position >= BAND - 1 + FRONT))

    update_mask = inside_rest(pos_home) & inside_rest(pos_other)
    pick_home = (pos_home[:, None] == jnp.arange(window_len)[None, :]).astype(jnp.float32)
    pick_other = (pos_other[:, None] == jnp.arange(window_len)[None, :]).astype(jnp.float32)
    rows_home = jnp.einsum("sp,pra->sra", pick_home, panel_blocks, precision=PRECISE)
    rows_other = jnp.einsum("sp,pra->sra", pick_other, panel_blocks, precision=PRECISE)
    change = jnp.einsum("sra,sca->src", rows_home, rows_other, precision=PRECISE)
    tiles_out = owned - jnp.where(update_mask[:, None, None], change, 0.0)
    solved_front = jax.scipy.linalg.solve_triangular(
        factor, window_rhs[BAND - 1 : BAND - 1 + FRONT].reshape(FRONT * cam_rows), lower=True
    )
    my_row = lax.dynamic_index_in_dim(
        panel_blocks, jnp.clip(my_pos, 0, window_len - 1), 0, keepdims=False
    )
    correction = reduced[0] - jnp.dot(my_row, solved_front, precision=PRECISE)
    front_piece = lax.dynamic_index_in_dim(
        solved_front.reshape(FRONT, cam_rows),
        jnp.clip(my_pos - (BAND - 1), 0, FRONT - 1),
        0,
        keepdims=False,
    )
    in_front = (my_pos >= BAND - 1) & (my_pos < BAND - 1 + FRONT)
    in_window = my_pos < window_len
    rhs_out = jnp.where(in_front, front_piece, jnp.where(in_window, correction, reduced[0]))[
        None, :
    ]
    return (tiles_out, rhs_out, front_panel)


def solution(mesh):
    in_specs = (
        P(("pts", "grp"), None, None, None, None),
        P(("pts", "grp"), None, None),
        P(("pts", "grp"), None, None),
        P(("pts", "grp"), None),
        P(),
        P(("pts", "grp"), None),
        P(),
        P(),
    )
    out_specs = (P(("pts", "grp"), None, None), P(("pts", "grp"), None), P(None, "grp"))
    return jax.shard_map(
        per_device, mesh=mesh, in_specs=in_specs, out_specs=out_specs, check_vma=False
    )
```

profile of v0, /device:TPU:0, one launch (start us, length us, event | category | flops | bytes accessed | tf_op | source)
XLA Modules:
  0.0 489.5 jit_solution(7508762552952673536)
XLA Ops:
  18.5 3.5 convolution_bitcast_fusion
  22.0 2.9 gather_fusion
  27.1 4.4 all-to-all-start
  32.1 5.0 %fusion.120 = s32[60]{0:T(128)S(1)} fusion(s32[60]{0:T(128)S(1)} %copy-done.16, s32[60]{0:T(128)S(1)} %copy-done.15, s32[]{:T(128)} %bitcast.1, s32[]{:T(128)} %bitcast.2, s32[]{:T(128)} %bitcast.3, s32[]{:T(128)} %bitcast.4, s32[]{:T(128)} %bitcast.5, s32[]{:T(128)} %bitcast.6, s32[]{:T(128)} %bitcast.7, s32[]{:T(128)} %bitcast.8, s32[]{:T(128)S(6)} %mul.589), kind=kLoop, calls=%fused_computation.234 | loop fusion | flops 1860 | bytes 756 | tf_op jit(solution)/shard_map/add | solution.py:68
  37.1 25.7 %all-to-all-done = f32[36,128,128]{2,0,1:T(8,128)S(1)} async-done(((f32[36,128,128]{2,0,1:T(8,128)}), f32[36,128,128]{2,0,1:T(8,128)S(1)}, u32[]{:S(2)}, u32[]{:S(2)}) %all-to-all-start) | async-done | bytes 2359328 | tf_op jit(solution)/shard_map/all_to_all | solution.py:129
  63.3 2.7 fusion.12
  68.2 6.6 %all-to-all-start.1 = ((f32[88,32,128]{2,1,0:T(8,128)}), f32[88,32,128]{2,1,0:T(8,128)S(1)}, u32[]{:S(2)}, u32[]{:S(2)}) async-start(f32[88,32,128]{2,1,0:T(8,128)} %copy.52), calls=%async_computation.1 | async-start | bytes 2883584 | tf_op jit(solution)/shard_map/all_to_all | solution.py:146
  78.3 30.5 %all-to-all-done.1 = f32[88,32,128]{2,1,0:T(8,128)S(1)} async-done(((f32[88,32,128]{2,1,0:T(8,128)}), f32[88,32,128]{2,1,0:T(8,128)S(1)}, u32[]{:S(2)}, u32[]{:S(2)}) %all-to-all-start.1) | async-done | bytes 1441824 | tf_op jit(solution)/shard_map/all_to_all | solution.py:146
  111.3 3.5 all-to-all-start.2
  114.8 10.1 %all-reduce.4.cloned.1.call-start = ((), (), s32[]{:S(2)}) async-start(), calls=%async_computation.3 | async-start | bytes 7864320 | tf_op jit(solution)/shard_map/psum | solution.py:192
  130.2 3.1 copy.58
  134.7 3.5 fusion.148
  151.3 38.8 %psum.15 = f32[18,128]{1,0:T(8,128)S(1)} all-reduce(f32[18,128]{1,0:T(8,128)S(1)} %broadcast_multiply_fusion), channel_id=1, replica_groups=mesh['pts'=8,'grp'=4] {'pts','grp'}, use_global_device_ids=true, to_apply=%region_10.11 | all-reduce | flops 2304 | bytes 18432 | tf_op jit(solution)/shard_map/psum | solution.py:192
  190.1 83.9 %all-reduce.4.cloned.1.call-done = f32[60,128,128]{2,1,0:T(8,128)} async-done(((f32[60,128,128]{2,1,0:T(8,128)}), f32[60,128,128]{2,1,0:T(8,128)}) %all-reduce.4.cloned.1.call-update) | async-done | bytes 3932176 | tf_op jit(solution)/shard_map/psum | solution.py:192
  274.0 4.5 concatenate.34
  278.5 5.2 %gather_fusion.1 = f32[72,128,128]{2,1,0:T(8,128)} fusion(f32[61,128,128]{2,1,0:T(8,128)} %concatenate.34, s32[1024]{0:T(1024)S(1)} %pad_clamp_fusion), kind=kCustom, calls=%fused_computation.1 | custom fusion | bytes 9437472 | tf_op jit(solution)/shard_map/gather | solution.py:206
  289.2 11.7 %cholesky.86 = f32[128,128]{1,0:T(8,128)S(1)} custom-call(f32[128,128]{1,0:T(8,128)S(1)} %cholesky.232), custom_call_target="Cholesky" | custom-call | tf_op jit(solution)/shard_map/jit(cholesky)/cholesky | solution.py:211
  301.1 6.5 %copy.75 = f32[18,128,4,128]{1,0,3,2:T(8,128)} copy(f32[18,128,4,128]{3,1,2,0:T(8,128)} %bitcast.269) | data formatting | bytes 9437184 | tf_op jit(solution)/shard_map/reshape | solution.py:208
  307.6 9.8 %custom-call.34 = f32[1,128,128]{1,2,0:T(8,128)S(1)} custom-call(f32[1,128,128]{2,1,0:T(8,128)S(1)} %get-tuple-element.50), custom_call_target="InvertDiagBlocksLowerTriangular" | custom-call | tf_op jit(solution)/shard_map/jit(cholesky)/cholesky | solution.py:211
  318.1 11.7 %cholesky.183 = f32[128,128]{1,0:T(8,128)S(1)} custom-call(f32[128,128]{1,0:T(8,128)S(1)} %cholesky.236), custom_call_target="Cholesky" | custom-call | tf_op jit(solution)/shard_map/jit(cholesky)/cholesky | solution.py:211
  331.2 9.8 %custom-call.35 = f32[1,128,128]{1,2,0:T(8,128)S(1)} custom-call(f32[1,128,128]{2,1,0:T(8,128)S(1)} %get-tuple-element.47), custom_call_target="InvertDiagBlocksLowerTriangular" | custom-call | tf_op jit(solution)/shard_map/jit(cholesky)/cholesky | solution.py:211
  341.6 12.1 %cholesky.204 = f32[128,128]{1,0:T(8,128)S(1)} custom-call(f32[128,128]{1,0:T(8,128)S(1)} %cholesky.241), custom_call_target="Cholesky" | custom-call | tf_op jit(solution)/shard_map/jit(cholesky)/cholesky | solution.py:211
  354.4 9.8 %custom-call.36 = f32[1,128,128]{1,2,0:T(8,128)S(1)} custom-call(f32[1,128,128]{2,1,0:T(8,128)S(1)} %get-tuple-element.44), custom_call_target="InvertDiagBlocksLowerTriangular" | custom-call | tf_op jit(solution)/shard_map/jit(cholesky)/cholesky | solution.py:211
  364.8 11.7 %cholesky.221 = f32[128,128]{1,0:T(8,128)S(1)} custom-call(f32[128,128]{1,0:T(8,128)S(1)} %convolution_subtract_fusion.5), custom_call_target="Cholesky" | custom-call | tf_op jit(solution)/shard_map/jit(cholesky)/cholesky | solution.py:211
  379.9 8.0 %while.1 = (s32[]{:T(128)}, f32[512,512]{1,0:T(8,128)S(1)}, s32[4,2]{0,1:T(2,128)S(1)}, f32[4,128,128]{2,1,0:T(8,128)S(1)}, s32[]{:T(128)}) while((s32[]{:T(128)}, f32[512,512]{1,0:T(8,128)S(1)}, s32[4,2]{0,1:T(2,128)S(1)}, f32[4,128,128]{2,1,0:T(8,128)S(1)}, s32[]{:T(128)}) %tuple.64), condition=%wide.while_cond, body=%wide.while_body.sunk | while | flops 2 | bytes 131181 | solution.py:212
  387.9 39.5 %custom-call.37 = f32[4,128,128]{1,2,0:T(8,128)S(1)} custom-call(f32[4,128,128]{2,1,0:T(8,128)S(1)} %get-tuple-element.10), custom_call_target="InvertDiagBlocksLowerTriangular" | custom-call | tf_op jit(solution)/shard_map/jit(_solve_triangular)/triangular_solve | solution.py:212
  427.4 3.8 copy.113
  440.6 4.3 pad_maximum_fusion
  444.9 6.1 %copy.63 = f32[2304,512]{1,0:T(8,128)} copy(f32[2304,512]{0,1:T(8,128)} %get-tuple-element.37) | data formatting | bytes 9437184 | tf_op jit(solution)/shard_map/transpose | solution.py:212
  451.0 7.7 %fusion.2 = f32[8,128,512]{2,0,1:T(8,128)S(1)} fusion(f32[18,128,512]{2,1,0:T(8,128)} %bitcast.264, s32[8]{0:T(128)S(1)} %get-tuple-element.30), kind=kOutput, calls=%fused_computation.6 | convolution fusion | flops 113246352 | bytes 6815776 | tf_op jit(solution)/shard_map/sp,pra->sra/dot_general | solution.py:223
  458.6 5.9 %fusion = f32[8,128,512]{2,0,1:T(8,128)} fusion(f32[18,128,512]{2,1,0:T(8,128)S(1)} %bitcast.266, s32[8]{0:T(128)S(1)} %get-tuple-element.29), kind=kOutput, calls=%fused_computation.4 | convolution fusion | flops 113246352 | bytes 6815776 | tf_op jit(solution)/shard_map/sp,pra->sra/dot_general | solution.py:224
  473.8 6.7 %fusion.28 = f32[8,128,128]{2,1,0:T(8,128)} fusion(f32[8,128,128]{2,1,0:T(8,128)S(1)} %bitcast_add_fusion.2, f32[8,128,512]{2,0,1:T(8,128)} %fusion, f32[8,128,512]{2,0,1:T(8,128)S(1)} %fusion.2, pred[8]{0:T(512)(128)(4,1)S(1)} %get-tuple-element.28), kind=kOutput, calls=%fused_computation.37 | convolution fusion | flops 805568512 | bytes 5242888 | tf_op jit(solution)/shard_map/sra,sca->src/dot_general | solution.py:225
  (150 shorter events, 80.4 us)
Async XLA Ops:
  7.2 118.4 %copy-start = (f32[32,128]{1,0:T(8,128)S(1)}, f32[32,128]{1,0:T(8,128)}, u32[]{:S(2)}) copy-start(f32[32,128]{1,0:T(8,128)} %param.21) | copy-start | bytes 49156
  13.8 2.0 copy-start.17
  15.8 1.4 copy-start.5
  17.2 1.2 copy-start.3
  18.5 3.5 copy-start.9
  27.1 4.4 copy-start.11
  27.1 5.0 %copy-start.15 = (s32[60]{0:T(128)S(1)}, s32[60]{0:T(128)}, u32[]{:S(2)}) copy-start(s32[60]{0:T(128)} %constant.368.clone) | copy-start | bytes 724
  27.1 5.0 %copy-start.16 = (s32[60]{0:T(128)S(1)}, s32[60]{0:T(128)}, u32[]{:S(2)}) copy-start(s32[60]{0:T(128)} %constant.369.clone) | copy-start | bytes 724
  27.1 35.7 %all-to-all-start = ((f32[36,128,128]{2,0,1:T(8,128)}), f32[36,128,128]{2,0,1:T(8,128)S(1)}, u32[]{:S(2)}, u32[]{:S(2)}) async-start(f32[36,128,128]{2,0,1:T(8,128)} %copy.49), calls=%async_computation | async-start | bytes 5242880 | tf_op jit(solution)/shard_map/all_to_all | solution.py:129
  37.1 26.2 %copy-start.10 = (f32[60,144,1]{1,0,2:T(8,128)S(1)}, f32[60,144,1]{1,0,2:T(8,128)}, u32[]{:S(2)}) copy-start(f32[60,144,1]{1,0,2:T(8,128)} %constant.431) | copy-start | bytes 103684
  68.2 40.5 %all-to-all-start.1 = ((f32[88,32,128]{2,1,0:T(8,128)}), f32[88,32,128]{2,1,0:T(8,128)S(1)}, u32[]{:S(2)}, u32[]{:S(2)}) async-start(f32[88,32,128]{2,1,0:T(8,128)} %copy.52), calls=%async_computation.1 | async-start | bytes 2883584 | tf_op jit(solution)/shard_map/all_to_all | solution.py:146
  111.3 14.4 %all-to-all-start.2 = ((f32[32,32,128]{2,1,0:T(8,128)}), f32[32,32,128]{2,1,0:T(8,128)S(1)}, u32[]{:S(2)}, u32[]{:S(2)}) async-start(f32[32,32,128]{2,1,0:T(8,128)} %copy.54), calls=%async_computation.2 | async-start | bytes 1048576 | tf_op jit(solution)/shard_map/all_to_all | solution.py:157
  114.8 159.2 %all-reduce.4.cloned.1.call-start = ((), (), s32[]{:S(2)}) async-start(), calls=%async_computation.3 | async-start | bytes 7864320 | tf_op jit(solution)/shard_map/psum | solution.py:192
  133.3 0.7 copy-start.12
  133.3 1.4 copy-start.4
  133.9 8.4 %copy-start.14 = (s32[72]{0:T(128)S(1)}, s32[72]{0:T(128)}, u32[]{:S(2)}) copy-start(s32[72]{0:T(128)} %constant.430) | copy-start | bytes 868
  133.9 17.3 %copy-start.13 = (f32[1,128]{1,0:T(1,128)S(1)}, f32[1,128]{1,0:T(1,128)}, u32[]{:S(2)}) copy-start(f32[1,128]{1,0:T(1,128)} %param.20) | copy-start | bytes 1540
  138.3 6.6 %collective-permute-start = (f32[128]{0:T(128)S(1)}, f32[128]{0:T(128)S(1)}, u32[]{:S(2)}, u32[]{:S(2)}) collective-permute-start(f32[128]{0:T(128)S(1)} %get-tuple-element.57), channel_id=1, source_target_pairs={{0,1},{1,2},{2,3},{3,4},{4,5},{5,6},{6,7},{7,8},{8,9},{9,10},{10,1... | collective-permute-start | bytes 1544 | tf_op jit(solution)/shard_map/ppermute | solution.py:16
  138.5 7.3 %collective-permute-start.1 = (f32[128]{0:T(128)S(1)}, f32[128]{0:T(128)S(1)}, u32[]{:S(2)}, u32[]{:S(2)}) collective-permute-start(f32[128]{0:T(128)S(1)} %get-tuple-element.63), channel_id=1, source_target_pairs={{0,2},{1,3},{2,4},{3,5},{4,6},{5,7},{6,8},{7,9},{8,10},{9,11},{10,... | collective-permute-start | bytes 1544 | tf_op jit(solution)/shard_map/ppermute | solution.py:16
  140.1 7.4 %collective-permute-start.2 = (f32[128]{0:T(128)S(1)}, f32[128]{0:T(128)S(1)}, u32[]{:S(2)}, u32[]{:S(2)}) collective-permute-start(f32[128]{0:T(128)S(1)} %get-tuple-element.62), channel_id=1, source_target_pairs={{0,3},{1,4},{2,5},{3,6},{4,7},{5,8},{6,9},{7,10},{8,11},{9,12},{10... | collective-permute-start | bytes 1544 | tf_op jit(solution)/shard_map/ppermute | solution.py:16
  142.3 6.3 %collective-permute-start.3 = (f32[128]{0:T(128)S(1)}, f32[128]{0:T(128)S(1)}, u32[]{:S(2)}, u32[]{:S(2)}) collective-permute-start(f32[128]{0:T(128)S(1)} %get-tuple-element.61), channel_id=1, source_target_pairs={{0,4},{1,5},{2,6},{3,7},{4,8},{5,9},{6,10},{7,11},{8,12},{9,13},{1... | collective-permute-start | bytes 1544 | tf_op jit(solution)/shard_map/ppermute | solution.py:16
  142.3 6.3 %collective-permute-start.4 = (f32[128]{0:T(128)S(1)}, f32[128]{0:T(128)S(1)}, u32[]{:S(2)}, u32[]{:S(2)}) collective-permute-start(f32[128]{0:T(128)S(1)} %get-tuple-element.60), channel_id=1, source_target_pairs={{0,5},{1,6},{2,7},{3,8},{4,9},{5,10},{6,11},{7,12},{8,13},{9,14},{... | collective-permute-start | bytes 1544 | tf_op jit(solution)/shard_map/ppermute | solution.py:16
  144.9 6.3 %collective-permute-start.5 = (f32[128]{0:T(128)S(1)}, f32[128]{0:T(128)S(1)}, u32[]{:S(2)}, u32[]{:S(2)}) collective-permute-start(f32[128]{0:T(128)S(1)} %get-tuple-element.59), channel_id=1, source_target_pairs={{0,6},{1,7},{2,8},{3,9},{4,10},{5,11},{6,12},{7,13},{8,14},{9,15},... | collective-permute-start | bytes 1544 | tf_op jit(solution)/shard_map/ppermute | solution.py:16
  145.8 5.4 %collective-permute-start.6 = (f32[128]{0:T(128)S(1)}, f32[128]{0:T(128)S(1)}, u32[]{:S(2)}, u32[]{:S(2)}) collective-permute-start(f32[128]{0:T(128)S(1)} %get-tuple-element.58), channel_id=1, source_target_pairs={{0,7},{1,8},{2,9},{3,10},{4,11},{5,12},{6,13},{7,14},{8,15},{9,16}... | collective-permute-start | bytes 1544 | tf_op jit(solution)/shard_map/ppermute | solution.py:16
  288.2 1.0 copy-start.7
  301.1 16.4 %copy-start.8 = (f32[512,512]{1,0:T(8,128)S(1)}, f32[512,512]{1,0:T(8,128)}, u32[]{:S(2)}) copy-start(f32[512,512]{1,0:T(8,128)} %copy-done.7) | copy-start | bytes 3145732
  387.9 49.3 %copy-start.6 = (f32[512,512]{1,0:T(8,128)}, f32[512,512]{1,0:T(8,128)S(1)}, u32[]{:S(2)}) copy-start(f32[512,512]{1,0:T(8,128)S(1)} %get-tuple-element.133) | copy-start | bytes 3145732
  451.0 7.7 %copy-start.2 = (f32[2304,512]{1,0:T(8,128)S(1)}, f32[2304,512]{1,0:T(8,128)}, u32[]{:S(2)}) copy-start(f32[2304,512]{1,0:T(8,128)} %copy.63) | copy-start | bytes 14155780
  473.8 8.5 %copy-start.1 = (f32[32,128]{1,0:T(8,128)S(1)}, f32[32,128]{1,0:T(8,128)}, u32[]{:S(2)}) copy-start(f32[32,128]{1,0:T(8,128)} %param.21) | copy-start | bytes 49156
Sparse Core Ops, SparseCore 0:
  133.4 140.5 all-reduce.3
where the time goes:
time: 499 us; the launch traced here: 490 us
  waiting for transfers between devices  147 us (29%)
  other arithmetic  134 us (27%)
  local copies, waits for them, and re-layouts  66.2 us (13%)
  matrix products  54.6 us (11%)
  blocking collectives  38.8 us (8%)
  starting transfers between devices  30.4 us (6%)
  between operations  18.1 us (4%)
    psum x1, waiting for transfers between devices, per_device(): front_rows, window_rhs = lax.psum((front_rows, window_rhs), ('pts', 'grp'))  83.9 us
    another operation x15, other arithmetic, per_device(): factor = jnp.linalg.cholesky(square)  79.4 us
    another operation x4, other arithmetic, per_device(): panel = jax.scipy.linalg.solve_triangular(factor, columns.T, lower=True).T  43.9 us
    psum x1, blocking collectives, per_device(): front_rows, window_rhs = lax.psum((front_rows, window_rhs), ('pts', 'grp'))  38.8 us
    all_to_all x1, waiting for transfers between devices, per_device(): lax.all_to_all(outgoing, 'pts', split_axis=0, concat_axis=0, tiled=True)  30.5 us
    all_to_all x1, waiting for transfers between devices, per_device(): lax.all_to_all(band_tiles, 'grp', split_axis=1, concat_axis=0, tiled=True)  25.7 us
    unnamed x40, local copies, waits for them, and re-layouts  13.1 us
    psum x1, starting transfers between devices, per_device(): front_rows, window_rhs = lax.psum((front_rows, window_rhs), ('pts', 'grp'))  10.1 us
  transfers between devices with their start and end apart: 11, of which 7 were waited for; matrix products, arithmetic and copies ran while one was open for 3% of the time, Pallas kernels for 0%

commit v1 on v0

--- a/solution.py
+++ b/solution.py
@@ -126,7 +126,10 @@
     perm_inverse = jnp.sum(jnp.arange(pts_count) * (tile_owner == my_pts))
     row_list, offset_list = band_table(BAND, BAND - 1)
     band_tiles = band_grid[row_list, row_list + offset_list]
-    quarters = lax.all_to_all(band_tiles, "grp", split_axis=1, concat_axis=0, tiled=True)
+    quarters = jnp.concatenate(
+        lax.all_to_all(jnp.stack(jnp.split(band_tiles, lax.axis_size("grp"), axis=1)), "grp", 0, 0),
+        axis=0,
+    )
     reach_union = BAND + grp_count - 2
     union_rows_list, union_offsets = band_table(reach_union + 1, reach_union)
     lookup = {}

time: 499 us -> 518 us (1.038)
  local copies, waits for them, and re-layouts: 66.2 us -> 77.1 us
    another operation x14 -> x19, local copies, waits for them, and re-layouts: 9.91 us -> 23.4 us  [the longest x5 13.5 us: per_device(): jnp.stack(jnp.split(band_tiles, lax.axis_size('grp'), axis=1))]
    all_to_all x1, starting transfers between devices: 6.65 us -> 17.8 us  [per_device(): lax.all_to_all(outgoing, 'pts', split_axis=0, concat_axis=0, tiled=True)]
    psum x1, starting transfers between devices: 10.1 us -> 0.04 us  [per_device(): front_rows, window_rhs = lax.psum((front_rows, window_rhs), ('pts', 'grp'))]
    all_to_all x1, waiting for transfers between devices: 0.01 us -> 7.85 us  [per_device(): lax.all_to_all(owner_rows, 'grp', split_axis=0, concat_axis=1, tiled=True)]
    unnamed x40 -> x44, local copies, waits for them, and re-layouts: 13.1 us -> 13 us
where the time goes in v1:
time: 518 us; the launch traced here: 508 us
  waiting for transfers between devices  152 us (29%)
  other arithmetic  137 us (26%)
  local copies, waits for them, and re-layouts  77.1 us (15%)
  matrix products  54.6 us (11%)
  blocking collectives  38.9 us (8%)
  starting transfers between devices  30.4 us (6%)
  between operations  18.2 us (4%)
    psum x1, waiting for transfers between devices, per_device(): front_rows, window_rhs = lax.psum((front_rows, window_rhs), ('pts', 'grp'))  82.6 us
    another operation x15, other arithmetic, per_device(): factor = jnp.linalg.cholesky(square)  79.1 us
    another operation x4, other arithmetic, per_device(): panel = jax.scipy.linalg.solve_triangular(factor, columns.T, lower=True).T  43.9 us
    psum x1, blocking collectives, per_device(): front_rows, window_rhs = lax.psum((front_rows, window_rhs), ('pts', 'grp'))  38.9 us
    all_to_all x1, waiting for transfers between devices, per_device(): lax.all_to_all(outgoing, 'pts', split_axis=0, concat_axis=0, tiled=True)  30.4 us
    all_to_all x1, waiting for transfers between devices, per_device(): lax.all_to_all(jnp.stack(jnp.split(band_tiles, lax.axis_size('grp'), axis...  22.6 us
    all_to_all x1, starting transfers between devices, per_device(): lax.all_to_all(outgoing, 'pts', split_axis=0, concat_axis=0, tiled=True)  17.8 us
    another operation x5, local copies, waits for them, and re-layouts, per_device(): jnp.stack(jnp.split(band_tiles, lax.axis_size('grp'), axis=1))  13.5 us
  transfers between devices with their start and end apart: 11, of which 7 were waited for; matrix products, arithmetic and copies ran while one was open for 3% of the time, Pallas kernels for 0%

profile of v1, /device:TPU:0, one launch (start us, length us, event | category | flops | bytes accessed | tf_op | source)
XLA Modules:
  0.0 508.2 jit_solution(16612316920199481232)
XLA Ops:
  18.4 3.5 convolution_bitcast_fusion
  24.8 5.6 %slice_bitcast_fusion.3 = (f32[1,36,32,128]{2,3,1,0:T(8,128)}, f32[1,36,32,128]{2,3,1,0:T(8,128)}, f32[1,36,32,128]{2,3,1,0:T(8,128)}, f32[1,36,32,128]{2,3,1,0:T(8,128)}) fusion(f32[36,128,128]{1,2,0:T(8,128)S(1)} %gather_fusion), kind=kLoop, calls=%fused_computation.22 | loop fusion | bytes 4718592 | tf_op jit(solution)/shard_map/stack | solution.py:130
  41.2 4.4 all-to-all-start
  46.3 5.2 %fusion.120 = s32[60]{0:T(128)S(1)} fusion(s32[60]{0:T(128)S(1)} %copy-done.18, s32[60]{0:T(128)S(1)} %copy-done.17, s32[]{:T(128)} %bitcast.1, s32[]{:T(128)} %bitcast.2, s32[]{:T(128)} %bitcast.3, s32[]{:T(128)} %bitcast.4, s32[]{:T(128)} %bitcast.5, s32[]{:T(128)} %bitcast.6, s32[]{:T(128)} %bitcast.7, s32[]{:T(128)} %bitcast.8, s32[]{:T(128)S(6)} %mul.589), kind=kLoop, calls=%fused_computation.239 | loop fusion | flops 1860 | bytes 756 | tf_op jit(solution)/shard_map/add | solution.py:68
  51.5 22.6 %all-to-all-done = f32[4,36,32,128]{3,2,1,0:T(8,128)S(1)} async-done(((f32[4,36,32,128]{3,2,1,0:T(8,128)}), f32[4,36,32,128]{3,2,1,0:T(8,128)S(1)}, u32[]{:S(2)}, u32[]{:S(2)}) %all-to-all-start) | async-done | bytes 2359328 | tf_op jit(solution)/shard_map/all_to_all | solution.py:130
  79.1 17.8 %all-to-all-start.1 = ((f32[88,32,128]{2,1,0:T(8,128)}), f32[88,32,128]{2,1,0:T(8,128)S(1)}, u32[]{:S(2)}, u32[]{:S(2)}) async-start(f32[88,32,128]{2,1,0:T(8,128)} %copy.81), calls=%async_computation.1 | async-start | bytes 2883584 | tf_op jit(solution)/shard_map/all_to_all | solution.py:149
  100.2 30.4 %all-to-all-done.1 = f32[88,32,128]{2,1,0:T(8,128)S(1)} async-done(((f32[88,32,128]{2,1,0:T(8,128)}), f32[88,32,128]{2,1,0:T(8,128)S(1)}, u32[]{:S(2)}, u32[]{:S(2)}) %all-to-all-start.1) | async-done | bytes 1441824 | tf_op jit(solution)/shard_map/all_to_all | solution.py:149
  133.2 3.5 all-to-all-start.2
  137.6 7.9 %all-to-all-done.2 = f32[32,32,128]{2,1,0:T(8,128)S(1)} async-done(((f32[32,32,128]{2,1,0:T(8,128)}), f32[32,32,128]{2,1,0:T(8,128)S(1)}, u32[]{:S(2)}, u32[]{:S(2)}) %all-to-all-start.2) | async-done | bytes 524320 | tf_op jit(solution)/shard_map/all_to_all | solution.py:160
  154.4 3.5 fusion.148
  160.8 3.9 collective-permute-done
  167.3 3.7 collective-permute-done.5
  171.1 38.9 %psum.15 = f32[18,128]{1,0:T(8,128)S(1)} all-reduce(f32[18,128]{1,0:T(8,128)S(1)} %broadcast_multiply_fusion), channel_id=1, replica_groups=mesh['pts'=8,'grp'=4] {'pts','grp'}, use_global_device_ids=true, to_apply=%region_10.11 | all-reduce | flops 2304 | bytes 18432 | tf_op jit(solution)/shard_map/psum | solution.py:195
  210.0 82.6 %all-reduce.4.cloned.1.call-done = f32[60,128,128]{2,1,0:T(8,128)} async-done(((f32[60,128,128]{2,1,0:T(8,128)}), f32[60,128,128]{2,1,0:T(8,128)}) %all-reduce.4.cloned.1.call-update) | async-done | bytes 3932176 | tf_op jit(solution)/shard_map/psum | solution.py:195
  292.6 4.5 concatenate.34
  297.1 5.2 %gather_fusion.1 = f32[72,128,128]{2,1,0:T(8,128)} fusion(f32[61,128,128]{2,1,0:T(8,128)} %concatenate.34, s32[1024]{0:T(1024)S(1)} %pad_clamp_fusion), kind=kCustom, calls=%fused_computation.1 | custom fusion | bytes 9437472 | tf_op jit(solution)/shard_map/gather | solution.py:209
  307.8 11.7 %cholesky.86 = f32[128,128]{1,0:T(8,128)S(1)} custom-call(f32[128,128]{1,0:T(8,128)S(1)} %cholesky.232), custom_call_target="Cholesky" | custom-call | tf_op jit(solution)/shard_map/jit(cholesky)/cholesky | solution.py:214
  319.7 6.7 %copy.104 = f32[18,128,4,128]{1,0,3,2:T(8,128)} copy(f32[18,128,4,128]{3,1,2,0:T(8,128)} %bitcast.277) | data formatting | bytes 9437184 | tf_op jit(solution)/shard_map/reshape | solution.py:211
  326.5 9.8 %custom-call.34 = f32[1,128,128]{1,2,0:T(8,128)S(1)} custom-call(f32[1,128,128]{2,1,0:T(8,128)S(1)} %get-tuple-element.57), custom_call_target="InvertDiagBlocksLowerTriangular" | custom-call | tf_op jit(solution)/shard_map/jit(cholesky)/cholesky | solution.py:214
  337.0 11.7 %cholesky.183 = f32[128,128]{1,0:T(8,128)S(1)} custom-call(f32[128,128]{1,0:T(8,128)S(1)} %cholesky.236), custom_call_target="Cholesky" | custom-call | tf_op jit(solution)/shard_map/jit(cholesky)/cholesky | solution.py:214
  350.0 9.8 %custom-call.35 = f32[1,128,128]{1,2,0:T(8,128)S(1)} custom-call(f32[1,128,128]{2,1,0:T(8,128)S(1)} %get-tuple-element.54), custom_call_target="InvertDiagBlocksLowerTriangular" | custom-call | tf_op jit(solution)/shard_map/jit(cholesky)/cholesky | solution.py:214
  360.5 11.9 %cholesky.204 = f32[128,128]{1,0:T(8,128)S(1)} custom-call(f32[128,128]{1,0:T(8,128)S(1)} %cholesky.241), custom_call_target="Cholesky" | custom-call | tf_op jit(solution)/shard_map/jit(cholesky)/cholesky | solution.py:214
  373.0 9.8 %custom-call.36 = f32[1,128,128]{1,2,0:T(8,128)S(1)} custom-call(f32[1,128,128]{2,1,0:T(8,128)S(1)} %get-tuple-element.51), custom_call_target="InvertDiagBlocksLowerTriangular" | custom-call | tf_op jit(solution)/shard_map/jit(cholesky)/cholesky | solution.py:214
  383.5 11.7 %cholesky.221 = f32[128,128]{1,0:T(8,128)S(1)} custom-call(f32[128,128]{1,0:T(8,128)S(1)} %convolution_subtract_fusion.5), custom_call_target="Cholesky" | custom-call | tf_op jit(solution)/shard_map/jit(cholesky)/cholesky | solution.py:214
  398.5 8.0 %while.1 = (s32[]{:T(128)}, f32[512,512]{1,0:T(8,128)S(1)}, s32[4,2]{0,1:T(2,128)S(1)}, f32[4,128,128]{2,1,0:T(8,128)S(1)}, s32[]{:T(128)}) while((s32[]{:T(128)}, f32[512,512]{1,0:T(8,128)S(1)}, s32[4,2]{0,1:T(2,128)S(1)}, f32[4,128,128]{2,1,0:T(8,128)S(1)}, s32[]{:T(128)}) %tuple.68), condition=%wide.while_cond, body=%wide.while_body.sunk | while | flops 2 | bytes 131181 | solution.py:215
  406.5 39.5 %custom-call.37 = f32[4,128,128]{1,2,0:T(8,128)S(1)} custom-call(f32[4,128,128]{2,1,0:T(8,128)S(1)} %get-tuple-element.10), custom_call_target="InvertDiagBlocksLowerTriangular" | custom-call | tf_op jit(solution)/shard_map/jit(_solve_triangular)/triangular_solve | solution.py:215
  446.0 3.8 copy.142
  459.3 4.3 pad_maximum_fusion
  463.5 6.1 %copy.92 = f32[2304,512]{1,0:T(8,128)} copy(f32[2304,512]{0,1:T(8,128)} %get-tuple-element.40) | data formatting | bytes 9437184 | tf_op jit(solution)/shard_map/transpose | solution.py:215
  469.6 7.7 %fusion.2 = f32[8,128,512]{2,0,1:T(8,128)S(1)} fusion(f32[18,128,512]{2,1,0:T(8,128)} %bitcast.272, s32[8]{0:T(128)S(1)} %get-tuple-element.33), kind=kOutput, calls=%fused_computation.6 | convolution fusion | flops 113246352 | bytes 6815776 | tf_op jit(solution)/shard_map/sp,pra->sra/dot_general | solution.py:226
  477.3 5.9 %fusion = f32[8,128,512]{2,0,1:T(8,128)} fusion(f32[18,128,512]{2,1,0:T(8,128)S(1)} %bitcast.274, s32[8]{0:T(128)S(1)} %get-tuple-element.32), kind=kOutput, calls=%fused_computation.4 | convolution fusion | flops 113246352 | bytes 6815776 | tf_op jit(solution)/shard_map/sp,pra->sra/dot_general | solution.py:227
  492.4 6.7 %fusion.28 = f32[8,128,128]{2,1,0:T(8,128)} fusion(f32[8,128,128]{2,1,0:T(8,128)S(1)} %bitcast_add_fusion.2, f32[8,128,512]{2,0,1:T(8,128)} %fusion, f32[8,128,512]{2,0,1:T(8,128)S(1)} %fusion.2, pred[8]{0:T(512)(128)(4,1)S(1)} %get-tuple-element.31), kind=kOutput, calls=%fused_computation.42 | convolution fusion | flops 805568512 | bytes 5242888 | tf_op jit(solution)/shard_map/sra,sca->src/dot_general | solution.py:228
  (158 shorter events, 89.6 us)
Async XLA Ops:
  7.2 130.3 %copy-start = (f32[32,128]{1,0:T(8,128)S(1)}, f32[32,128]{1,0:T(8,128)}, u32[]{:S(2)}) copy-start(f32[32,128]{1,0:T(8,128)} %param.21) | copy-start | bytes 49156
  11.7 4.1 copy-start.19
  15.8 1.4 copy-start.7
  17.2 1.1 copy-start.5
  18.4 3.5 copy-start.11
  30.4 2.5 copy-start.4
  33.5 3.3 copy-start.3
  41.2 4.4 copy-start.13
  41.2 5.1 copy-start.17
  41.2 5.1 copy-start.18
  41.2 32.9 %copy-start.12 = (f32[60,144,1]{1,0,2:T(8,128)S(1)}, f32[60,144,1]{1,0,2:T(8,128)}, u32[]{:S(2)}) copy-start(f32[60,144,1]{1,0,2:T(8,128)} %constant.428) | copy-start | bytes 103684
  41.2 32.9 %all-to-all-start = ((f32[4,36,32,128]{3,2,1,0:T(8,128)}), f32[4,36,32,128]{3,2,1,0:T(8,128)S(1)}, u32[]{:S(2)}, u32[]{:S(2)}) async-start(f32[4,36,32,128]{3,2,1,0:T(8,128)} %pad_maximum_fusion.1), calls=%async_computation | async-start | bytes 4718592 | tf_op jit(solution)/shard_map/all_to_all | solution.py:130
  79.1 51.6 %all-to-all-start.1 = ((f32[88,32,128]{2,1,0:T(8,128)}), f32[88,32,128]{2,1,0:T(8,128)S(1)}, u32[]{:S(2)}, u32[]{:S(2)}) async-start(f32[88,32,128]{2,1,0:T(8,128)} %copy.81), calls=%async_computation.1 | async-start | bytes 2883584 | tf_op jit(solution)/shard_map/all_to_all | solution.py:149
  133.2 12.3 %all-to-all-start.2 = ((f32[32,32,128]{2,1,0:T(8,128)}), f32[32,32,128]{2,1,0:T(8,128)S(1)}, u32[]{:S(2)}, u32[]{:S(2)}) async-start(f32[32,32,128]{2,1,0:T(8,128)} %copy.83), calls=%async_computation.2 | async-start | bytes 1048576 | tf_op jit(solution)/shard_map/all_to_all | solution.py:160
  136.7 155.9 %all-reduce.4.cloned.1.call-start = ((), (), s32[]{:S(2)}) async-start(), calls=%async_computation.3 | async-start | bytes 7864320 | tf_op jit(solution)/shard_map/psum | solution.py:195
  153.0 0.7 copy-start.14
  153.0 1.4 copy-start.6
  153.0 7.8 %copy-start.16 = (s32[72]{0:T(128)S(1)}, s32[72]{0:T(128)}, u32[]{:S(2)}) copy-start(s32[72]{0:T(128)} %constant.427) | copy-start | bytes 868
  153.0 18.1 %copy-start.15 = (f32[1,128]{1,0:T(1,128)S(1)}, f32[1,128]{1,0:T(1,128)}, u32[]{:S(2)}) copy-start(f32[1,128]{1,0:T(1,128)} %param.20) | copy-start | bytes 1540
  158.0 6.7 %collective-permute-start = (f32[128]{0:T(128)S(1)}, f32[128]{0:T(128)S(1)}, u32[]{:S(2)}, u32[]{:S(2)}) collective-permute-start(f32[128]{0:T(128)S(1)} %get-tuple-element.64), channel_id=1, source_target_pairs={{0,1},{1,2},{2,3},{3,4},{4,5},{5,6},{6,7},{7,8},{8,9},{9,10},{10,1... | collective-permute-start | bytes 1544 | tf_op jit(solution)/shard_map/ppermute | solution.py:16
  158.1 7.2 %collective-permute-start.1 = (f32[128]{0:T(128)S(1)}, f32[128]{0:T(128)S(1)}, u32[]{:S(2)}, u32[]{:S(2)}) collective-permute-start(f32[128]{0:T(128)S(1)} %get-tuple-element.70), channel_id=1, source_target_pairs={{0,2},{1,3},{2,4},{3,5},{4,6},{5,7},{6,8},{7,9},{8,10},{9,11},{10,... | collective-permute-start | bytes 1544 | tf_op jit(solution)/shard_map/ppermute | solution.py:16
  158.5 8.8 %collective-permute-start.2 = (f32[128]{0:T(128)S(1)}, f32[128]{0:T(128)S(1)}, u32[]{:S(2)}, u32[]{:S(2)}) collective-permute-start(f32[128]{0:T(128)S(1)} %get-tuple-element.69), channel_id=1, source_target_pairs={{0,3},{1,4},{2,5},{3,6},{4,7},{5,8},{6,9},{7,10},{8,11},{9,12},{10... | collective-permute-start | bytes 1544 | tf_op jit(solution)/shard_map/ppermute | solution.py:16
  160.8 6.5 %collective-permute-start.3 = (f32[128]{0:T(128)S(1)}, f32[128]{0:T(128)S(1)}, u32[]{:S(2)}, u32[]{:S(2)}) collective-permute-start(f32[128]{0:T(128)S(1)} %get-tuple-element.68), channel_id=1, source_target_pairs={{0,4},{1,5},{2,6},{3,7},{4,8},{5,9},{6,10},{7,11},{8,12},{9,13},{1... | collective-permute-start | bytes 1544 | tf_op jit(solution)/shard_map/ppermute | solution.py:16
  160.8 6.5 %collective-permute-start.4 = (f32[128]{0:T(128)S(1)}, f32[128]{0:T(128)S(1)}, u32[]{:S(2)}, u32[]{:S(2)}) collective-permute-start(f32[128]{0:T(128)S(1)} %get-tuple-element.67), channel_id=1, source_target_pairs={{0,5},{1,6},{2,7},{3,8},{4,9},{5,10},{6,11},{7,12},{8,13},{9,14},{... | collective-permute-start | bytes 1544 | tf_op jit(solution)/shard_map/ppermute | solution.py:16
  164.8 6.3 %collective-permute-start.5 = (f32[128]{0:T(128)S(1)}, f32[128]{0:T(128)S(1)}, u32[]{:S(2)}, u32[]{:S(2)}) collective-permute-start(f32[128]{0:T(128)S(1)} %get-tuple-element.66), channel_id=1, source_target_pairs={{0,6},{1,7},{2,8},{3,9},{4,10},{5,11},{6,12},{7,13},{8,14},{9,15},... | collective-permute-start | bytes 1544 | tf_op jit(solution)/shard_map/ppermute | solution.py:16
  165.3 5.7 %collective-permute-start.6 = (f32[128]{0:T(128)S(1)}, f32[128]{0:T(128)S(1)}, u32[]{:S(2)}, u32[]{:S(2)}) collective-permute-start(f32[128]{0:T(128)S(1)} %get-tuple-element.65), channel_id=1, source_target_pairs={{0,7},{1,8},{2,9},{3,10},{4,11},{5,12},{6,13},{7,14},{8,15},{9,16}... | collective-permute-start | bytes 1544 | tf_op jit(solution)/shard_map/ppermute | solution.py:16
  306.9 1.0 copy-start.9
  319.7 16.6 %copy-start.10 = (f32[512,512]{1,0:T(8,128)S(1)}, f32[512,512]{1,0:T(8,128)}, u32[]{:S(2)}) copy-start(f32[512,512]{1,0:T(8,128)} %copy-done.9) | copy-start | bytes 3145732
  406.5 49.4 %copy-start.8 = (f32[512,512]{1,0:T(8,128)}, f32[512,512]{1,0:T(8,128)S(1)}, u32[]{:S(2)}) copy-start(f32[512,512]{1,0:T(8,128)S(1)} %get-tuple-element.140) | copy-start | bytes 3145732
  469.6 7.7 %copy-start.2 = (f32[2304,512]{1,0:T(8,128)S(1)}, f32[2304,512]{1,0:T(8,128)}, u32[]{:S(2)}) copy-start(f32[2304,512]{1,0:T(8,128)} %copy.92) | copy-start | bytes 14155780
  492.4 8.5 %copy-start.1 = (f32[32,128]{1,0:T(8,128)S(1)}, f32[32,128]{1,0:T(8,128)}, u32[]{:S(2)}) copy-start(f32[32,128]{1,0:T(8,128)} %param.21) | copy-start | bytes 49156
Sparse Core Ops, SparseCore 0:
  153.1 139.4 all-reduce.3
